TPU v7x, 512 devices: a whole 4x4x16 slice. The times are simulated.
512 devices in a mesh: spec: 16 (over y, x), tile: 32 (over z, core).
Axes of the slice: x: 4, y: 4, z: 16, core: 2. Of those that a mesh axis runs over, the one named last changes fastest.
Arguments:
- action: bfloat16 [512, 3072, 256], P('tile', 'spec'), may hold values from 0.099609375 to 2
- east_current: float32 [512, 256], P('tile'), may hold values from -0.4 to 0.4
- north_current: float32 [512, 256], P('tile'), may hold values from -0.4 to 0.4
- sea_mask: int32 [512, 256], P('tile'), may hold values from 0 to 1, as said below
- pattern: int32 [48, 24], replicated, may hold values from 0 to 47, as said below
- table: bfloat16 [48, 64, 64], replicated, may hold values from -0.15625 to 0.15625
Outputs:
- updated: bfloat16 [512, 3072, 256], P('tile', 'spec')
Inputs may be any that keep to these rules, and one draw needn't show every extreme that they name: `sea_mask`: each tile of 16 latitude rows (all 256 longitudes) holds at most 2048 sea points, and in every draw some tile holds exactly 2048. `pattern`: each row names 24 different direction blocks.
All inputs are finite; a program needn't handle non-finite values.
Results may differ from a plain program's by a relative error of at most 0.0043.
Values may be sent and summed in bfloat16 or wider, within the bound.
A program may use at most 64 MiB of HBM per device.

v0:
```python
import jax
import jax.numpy as jnp
from jax import lax
from jax.sharding import PartitionSpec as P

NF = 64
ND = 48
SUB = 2
courant_scale = 0.45


def extended(cells, sides, width):
    for axis, dim in sides:
        count = lax.axis_size(axis)
        ends = count - 1
        head = lax.slice_in_dim(cells, 0, width, axis=dim)
        tail = lax.slice_in_dim(cells, cells.shape[dim] - width, cells.shape[dim], axis=dim)
        cells = jnp.concatenate(
            [
                lax.ppermute(tail, axis, [(i, (i + 1) % count) for i in range(ends)]),
                cells,
                lax.ppermute(head, axis, [((i + 1) % count, i) for i in range(ends)]),
            ],
            axis=dim,
        )
    return cells


def upwind(padded, courant_east, courant_north):
    center = padded[1:-1]
    south_row = padded[:-2]
    north_row = padded[2:]
    zero_column = jnp.zeros_like(center[:, :, :1])
    west_cell = jnp.concatenate([zero_column, center[:, :, :-1]], axis=2)
    east_cell = jnp.concatenate([center[:, :, 1:], zero_column], axis=2)
    return (
        center
        - jnp.maximum(courant_east, 0.0) * (center - west_cell)
        - jnp.minimum(courant_east, 0.0) * (east_cell - center)
        - jnp.maximum(courant_north, 0.0) * (center - south_row)
        - jnp.minimum(courant_north, 0.0) * (north_row - center)
    )


def source_update(cell_action, cell_mask, pattern, table):
    row_count = cell_action.shape[0]
    lane_count = cell_action.shape[2]
    group_size = 8
    offsets = (pattern - jnp.arange(ND, dtype=jnp.int32)[:, None]) % ND
    directions = jnp.arange(ND, dtype=jnp.int32)

    def advance_group(unused_state, group_rows):
        selector = (pattern[group_rows][:, :, None] == directions[None, None, :]).astype(
            jnp.float32
        )
        weights = table[offsets[group_rows]].astype(jnp.float32)
        assembled = jnp.einsum("rjc,rjab->racb", selector, weights)
        assembled = assembled.astype(jnp.bfloat16).reshape(group_size * NF, ND * NF)
        coupled = jnp.einsum(
            "ak,rkl->ral", assembled, cell_action, preferred_element_type=jnp.float32
        )
        return (unused_state, coupled)

    group_index = directions.reshape(ND // group_size, group_size)
    unused_state, coupled = lax.scan(advance_group, jnp.zeros((), jnp.float32), group_index)
    coupled = jnp.transpose(coupled, (1, 0, 2, 3)).reshape(row_count, ND * NF, lane_count)
    own_action = cell_action.astype(jnp.float32)
    sea_part = cell_mask.astype(jnp.float32)[:, None, :]
    result = own_action + sea_part * own_action * coupled
    return result.astype(jnp.bfloat16)


def local(action, east_current, north_current, sea_mask, pattern, table):
    tile_rows = action.shape[0]
    comp_count = action.shape[1]
    spec_count = lax.axis_size("spec")
    spec_index = lax.axis_index("spec")
    components = spec_index * comp_count + jnp.arange(comp_count, dtype=jnp.int32)
    direction = (components // NF).astype(jnp.float32)
    frequency = (components % NF).astype(jnp.float32)
    speed = jnp.exp(-2.0 * frequency / (NF - 1))
    theta = 2.0 * jnp.pi * direction / ND
    courant_east = courant_scale * (
        (speed * jnp.cos(theta))[None, :, None] + east_current[:, None, :]
    )
    courant_north = courant_scale * (
        (speed * jnp.sin(theta))[None, :, None] + north_current[:, None, :]
    )
    field = action.astype(jnp.float32)
    for substep in range(SUB):
        padded = extended(field, (("tile", 0),), 1)
        field = upwind(padded, courant_east, courant_north)
    moved = field.astype(jnp.bfloat16)
    share_rows = tile_rows // spec_count
    incoming = lax.all_to_all(moved, "spec", split_axis=0, concat_axis=1, tiled=True)
    own_mask = lax.dynamic_slice_in_dim(sea_mask, spec_index * share_rows, share_rows, 0)
    renewed = source_update(incoming, own_mask, pattern, table)
    result = lax.all_to_all(renewed, "spec", split_axis=1, concat_axis=0, tiled=True)
    return result


def solution(mesh):
    return jax.shard_map(
        local,
        mesh=mesh,
        in_specs=(
            P("tile", "spec", None),
            P("tile", None),
            P("tile", None),
            P("tile", None),
            P(),
            P(),
        ),
        out_specs=P("tile", "spec", None),
        check_vma=False,
    )
```

profile of v0, /device:TPU:320, one launch (start us, length us, event | category | flops | bytes accessed | tf_op | source)
XLA Modules:
  0.0 262.7 jit_solution(9454348573724922030)
XLA Ops:
  0.0 1.0 fusion.42
  1.0 1.9 collective-permute-start
  2.9 3.8 %collective-permute-start.1 = (f32[1,192,256]{2,1,0:T(8,128)S(1)}, f32[1,192,256]{2,1,0:T(8,128)S(1)}, u32[]{:S(2)}, u32[]{:S(2)}) collective-permute-start(f32[1,192,256]{2,1,0:T(8,128)S(1)} %get-tuple-element.106), channel_id=1, source_target_pairs={{1,0},{2,1},{3,2},{4,3},{5,4},{6,5},{7,6},{8,7},{9,8},{10,9},{11,1... | collective-permute-start | bytes 589832 | tf_op jit(solution)/shard_map/ppermute | solution.py:22
  6.7 5.5 %fusion.41 = (f32[16,192,255]{2,1,0:T(8,128)}, f32[16,192,255]{2,1,0:T(8,128)}) fusion(bf16[16,192,256]{2,1,0:T(8,128)(2,1)} %param.8), kind=kLoop, calls=%fused_computation.71 | loop fusion | bytes 12533760 | tf_op jit(solution)/shard_map/slice | solution.py:34
  12.2 2.0 convert_element_type.59
  14.3 5.8 %fusion.18 = f32[16,192,256]{2,1,0:T(8,128)S(1)} fusion(bf16[16,192,256]{2,1,0:T(8,128)(2,1)S(1)} %copy-done, f32[1,192,256]{2,1,0:T(8,128)S(1)} %collective-permute-done.1, f32[16,192,256]{2,1,0:T(8,128)} %convert_element_type.59, f32[1,192,256]{2,1,0:T(8,128)S(1)} %collective-permute-done, f32[16,192,255]{2,1,0:T(8,128)} %get-tuple-element.104, ...), kind=kLoop, calls=%fused_computation.28 | loop fusion | flops 18087936 | bytes 14558720 | tf_op jit(solution)/shard_map/sub | solution.py:37
  20.1 1.9 collective-permute-start.2
  22.1 3.6 %collective-permute-start.3 = (f32[1,192,256]{2,1,0:T(8,128)S(1)}, f32[1,192,256]{2,1,0:T(8,128)S(1)}, u32[]{:S(2)}, u32[]{:S(2)}) collective-permute-start(f32[1,192,256]{2,1,0:T(8,128)S(1)} %get-tuple-element.102), channel_id=1, source_target_pairs={{1,0},{2,1},{3,2},{4,3},{5,4},{6,5},{7,6},{8,7},{9,8},{10,9},{11,1... | collective-permute-start | bytes 589832 | tf_op jit(solution)/shard_map/ppermute | solution.py:22
  25.7 1.2 fusion.39
  26.9 0.2 collective-permute-done.2
  27.1 1.8 collective-permute-done.3
  28.9 3.9 %fusion.27 = bf16[16,192,256]{2,1,0:T(8,128)(2,1)} fusion(f32[16,192,256]{2,1,0:T(8,128)S(1)} %fusion.18, f32[1,192,256]{2,1,0:T(8,128)S(1)} %collective-permute-done.3, f32[1,192,256]{2,1,0:T(8,128)S(1)} %collective-permute-done.2, f32[16,192,255]{2,1,0:T(8,128)S(1)} %get-tuple-element.100, f32[16,192,255]{2,1,0:T(8,128)S(1)} %get-tuple-element.99, ...), kind=kLoop, calls=%fused_computation.38 | loop fusion | flops 18087936 | bytes 11412992 | tf_op jit(solution)/shard_map/convert_element_type | solution.py:93
  32.8 7.2 %all-to-all-start = ((bf16[16,192,256]{2,1,0:T(8,128)(2,1)}), bf16[16,192,256]{2,1,0:T(8,128)(2,1)}, u32[]{:S(2)}, u32[]{:S(2)}) async-start(bf16[16,192,256]{2,1,0:T(8,128)(2,1)} %fusion.27), calls=%async_computation | async-start | bytes 3145728 | tf_op jit(solution)/shard_map/all_to_all | solution.py:95
  40.1 0.7 dynamic-slice_convert_fusion
  40.9 27.2 %all-to-all-done = bf16[16,192,256]{2,1,0:T(8,128)(2,1)} async-done(((bf16[16,192,256]{2,1,0:T(8,128)(2,1)}), bf16[16,192,256]{2,1,0:T(8,128)(2,1)}, u32[]{:S(2)}, u32[]{:S(2)}) %all-to-all-start) | async-done | bytes 1572896 | tf_op jit(solution)/shard_map/all_to_all | solution.py:95
  68.0 117.2 %while.11 = (s32[]{:T(128)}, f32[6,1,512,256]{3,2,1,0:T(8,128)}, s32[6,8]{1,0:T(8,128)S(1)}, s32[48,24]{1,0:T(8,128)S(1)}, bf16[48,64,64]{2,1,0:T(8,128)(2,1)}, ...) while((s32[]{:T(128)}, f32[6,1,512,256]{3,2,1,0:T(8,128)}, ...), condition=%wide.region_1.2_spmd.clone, body=%wide.region_0.1_spmd.clone.sunk | while | flops 882388544 | bytes 19416056 | solution.py:65
  68.1 0.6 gather_fusion
  68.6 0.1 reshape.228
  68.7 2.3 gather_fusion.1
  71.0 0.6 gather_fusion.2
  71.6 5.3 %convert_bitcast_fusion.2 = bf16[8,64,48,64]{3,2,1,0:T(8,128)(2,1)} fusion(bf16[8,24,64,64]{3,2,1,0:T(8,128)(2,1)S(1)} %bitcast.64, s32[8,24]{1,0:T(8,128)S(1)} %gather_fusion.2), kind=kOutput, calls=%fused_computation.4.clone.1 | convolution fusion | flops 77079552 | bytes 4719360 | tf_op jit(solution)/shard_map/while/body/eval_jaxpr/rjc,rjab->racb/dot_general | solution.py:57
  76.8 7.5 %reshape.229 = bf16[512,3072]{1,0:T(8,128)(2,1)S(1)} reshape(bf16[8,64,48,64]{3,2,1,0:T(8,128)(2,1)} %convert_bitcast_fusion.2) | data formatting | bytes 6291456 | tf_op jit(solution)/shard_map/while/body/eval_jaxpr/reshape | solution.py:58
  84.4 3.2 %fusion.55 = f32[6,1,512,256]{3,2,1,0:T(8,128)} fusion(f32[6,1,512,256]{3,2,1,0:T(8,128)} %get-tuple-element.161, s32[]{:T(128)} %get-tuple-element.160, bf16[512,3072]{1,0:T(8,128)(2,1)S(1)} %reshape.229, bf16[1,3072,256]{2,1,0:T(8,128)(2,1)} %get-tuple-element.174), kind=kOutput, calls=%fused_computation.9.clone.1 | convolution fusion | flops 805306368 | bytes 5243392 | tf_op jit(solution)/shard_map/while/body/eval_jaxpr/ak,rkl->ral/dot_general | solution.py:59
  87.6 0.6 gather_fusion
  88.1 0.1 reshape.228
  88.2 2.3 gather_fusion.1
  90.5 0.6 gather_fusion.2
  91.1 5.3 %convert_bitcast_fusion.2 = bf16[8,64,48,64]{3,2,1,0:T(8,128)(2,1)} fusion(bf16[8,24,64,64]{3,2,1,0:T(8,128)(2,1)S(1)} %bitcast.64, s32[8,24]{1,0:T(8,128)S(1)} %gather_fusion.2), kind=kOutput, calls=%fused_computation.4.clone.1 | convolution fusion | flops 77079552 | bytes 4719360 | tf_op jit(solution)/shard_map/while/body/eval_jaxpr/rjc,rjab->racb/dot_general | solution.py:57
  96.4 7.5 %reshape.229 = bf16[512,3072]{1,0:T(8,128)(2,1)S(1)} reshape(bf16[8,64,48,64]{3,2,1,0:T(8,128)(2,1)} %convert_bitcast_fusion.2) | data formatting | bytes 6291456 | tf_op jit(solution)/shard_map/while/body/eval_jaxpr/reshape | solution.py:58
  103.9 3.2 %fusion.55 = f32[6,1,512,256]{3,2,1,0:T(8,128)} fusion(f32[6,1,512,256]{3,2,1,0:T(8,128)} %get-tuple-element.161, s32[]{:T(128)} %get-tuple-element.160, bf16[512,3072]{1,0:T(8,128)(2,1)S(1)} %reshape.229, bf16[1,3072,256]{2,1,0:T(8,128)(2,1)} %get-tuple-element.174), kind=kOutput, calls=%fused_computation.9.clone.1 | convolution fusion | flops 805306368 | bytes 5243392 | tf_op jit(solution)/shard_map/while/body/eval_jaxpr/ak,rkl->ral/dot_general | solution.py:59
  107.1 0.6 gather_fusion
  107.6 0.1 reshape.228
  107.7 2.3 gather_fusion.1
  110.0 0.6 gather_fusion.2
  110.6 5.3 %convert_bitcast_fusion.2 = bf16[8,64,48,64]{3,2,1,0:T(8,128)(2,1)} fusion(bf16[8,24,64,64]{3,2,1,0:T(8,128)(2,1)S(1)} %bitcast.64, s32[8,24]{1,0:T(8,128)S(1)} %gather_fusion.2), kind=kOutput, calls=%fused_computation.4.clone.1 | convolution fusion | flops 77079552 | bytes 4719360 | tf_op jit(solution)/shard_map/while/body/eval_jaxpr/rjc,rjab->racb/dot_general | solution.py:57
  115.9 7.5 %reshape.229 = bf16[512,3072]{1,0:T(8,128)(2,1)S(1)} reshape(bf16[8,64,48,64]{3,2,1,0:T(8,128)(2,1)} %convert_bitcast_fusion.2) | data formatting | bytes 6291456 | tf_op jit(solution)/shard_map/while/body/eval_jaxpr/reshape | solution.py:58
  123.4 3.2 %fusion.55 = f32[6,1,512,256]{3,2,1,0:T(8,128)} fusion(f32[6,1,512,256]{3,2,1,0:T(8,128)} %get-tuple-element.161, s32[]{:T(128)} %get-tuple-element.160, bf16[512,3072]{1,0:T(8,128)(2,1)S(1)} %reshape.229, bf16[1,3072,256]{2,1,0:T(8,128)(2,1)} %get-tuple-element.174), kind=kOutput, calls=%fused_computation.9.clone.1 | convolution fusion | flops 805306368 | bytes 5243392 | tf_op jit(solution)/shard_map/while/body/eval_jaxpr/ak,rkl->ral/dot_general | solution.py:59
  126.6 0.6 gather_fusion
  127.2 2.3 gather_fusion.1
  129.5 0.6 gather_fusion.2
  130.1 5.3 %convert_bitcast_fusion.2 = bf16[8,64,48,64]{3,2,1,0:T(8,128)(2,1)} fusion(bf16[8,24,64,64]{3,2,1,0:T(8,128)(2,1)S(1)} %bitcast.64, s32[8,24]{1,0:T(8,128)S(1)} %gather_fusion.2), kind=kOutput, calls=%fused_computation.4.clone.1 | convolution fusion | flops 77079552 | bytes 4719360 | tf_op jit(solution)/shard_map/while/body/eval_jaxpr/rjc,rjab->racb/dot_general | solution.py:57
  135.4 7.5 %reshape.229 = bf16[512,3072]{1,0:T(8,128)(2,1)S(1)} reshape(bf16[8,64,48,64]{3,2,1,0:T(8,128)(2,1)} %convert_bitcast_fusion.2) | data formatting | bytes 6291456 | tf_op jit(solution)/shard_map/while/body/eval_jaxpr/reshape | solution.py:58
  142.9 3.2 %fusion.55 = f32[6,1,512,256]{3,2,1,0:T(8,128)} fusion(f32[6,1,512,256]{3,2,1,0:T(8,128)} %get-tuple-element.161, s32[]{:T(128)} %get-tuple-element.160, bf16[512,3072]{1,0:T(8,128)(2,1)S(1)} %reshape.229, bf16[1,3072,256]{2,1,0:T(8,128)(2,1)} %get-tuple-element.174), kind=kOutput, calls=%fused_computation.9.clone.1 | convolution fusion | flops 805306368 | bytes 5243392 | tf_op jit(solution)/shard_map/while/body/eval_jaxpr/ak,rkl->ral/dot_general | solution.py:59
  146.1 0.6 gather_fusion
  146.7 0.1 reshape.228
  146.8 2.3 gather_fusion.1
  149.1 0.6 gather_fusion.2
  149.6 5.3 %convert_bitcast_fusion.2 = bf16[8,64,48,64]{3,2,1,0:T(8,128)(2,1)} fusion(bf16[8,24,64,64]{3,2,1,0:T(8,128)(2,1)S(1)} %bitcast.64, s32[8,24]{1,0:T(8,128)S(1)} %gather_fusion.2), kind=kOutput, calls=%fused_computation.4.clone.1 | convolution fusion | flops 77079552 | bytes 4719360 | tf_op jit(solution)/shard_map/while/body/eval_jaxpr/rjc,rjab->racb/dot_general | solution.py:57
  154.9 7.5 %reshape.229 = bf16[512,3072]{1,0:T(8,128)(2,1)S(1)} reshape(bf16[8,64,48,64]{3,2,1,0:T(8,128)(2,1)} %convert_bitcast_fusion.2) | data formatting | bytes 6291456 | tf_op jit(solution)/shard_map/while/body/eval_jaxpr/reshape | solution.py:58
  162.4 3.2 %fusion.55 = f32[6,1,512,256]{3,2,1,0:T(8,128)} fusion(f32[6,1,512,256]{3,2,1,0:T(8,128)} %get-tuple-element.161, s32[]{:T(128)} %get-tuple-element.160, bf16[512,3072]{1,0:T(8,128)(2,1)S(1)} %reshape.229, bf16[1,3072,256]{2,1,0:T(8,128)(2,1)} %get-tuple-element.174), kind=kOutput, calls=%fused_computation.9.clone.1 | convolution fusion | flops 805306368 | bytes 5243392 | tf_op jit(solution)/shard_map/while/body/eval_jaxpr/ak,rkl->ral/dot_general | solution.py:59
  165.7 0.6 gather_fusion
  166.3 2.3 gather_fusion.1
  168.6 0.6 gather_fusion.2
  169.2 5.3 %convert_bitcast_fusion.2 = bf16[8,64,48,64]{3,2,1,0:T(8,128)(2,1)} fusion(bf16[8,24,64,64]{3,2,1,0:T(8,128)(2,1)S(1)} %bitcast.64, s32[8,24]{1,0:T(8,128)S(1)} %gather_fusion.2), kind=kOutput, calls=%fused_computation.4.clone.1 | convolution fusion | flops 77079552 | bytes 4719360 | tf_op jit(solution)/shard_map/while/body/eval_jaxpr/rjc,rjab->racb/dot_general | solution.py:57
  174.5 7.5 %reshape.229 = bf16[512,3072]{1,0:T(8,128)(2,1)S(1)} reshape(bf16[8,64,48,64]{3,2,1,0:T(8,128)(2,1)} %convert_bitcast_fusion.2) | data formatting | bytes 6291456 | tf_op jit(solution)/shard_map/while/body/eval_jaxpr/reshape | solution.py:58
  182.0 3.2 %fusion.55 = f32[6,1,512,256]{3,2,1,0:T(8,128)} fusion(f32[6,1,512,256]{3,2,1,0:T(8,128)} %get-tuple-element.161, s32[]{:T(128)} %get-tuple-element.160, bf16[512,3072]{1,0:T(8,128)(2,1)S(1)} %reshape.229, bf16[1,3072,256]{2,1,0:T(8,128)(2,1)} %get-tuple-element.174), kind=kOutput, calls=%fused_computation.9.clone.1 | convolution fusion | flops 805306368 | bytes 5243392 | tf_op jit(solution)/shard_map/while/body/eval_jaxpr/ak,rkl->ral/dot_general | solution.py:59
  185.2 2.8 %fusion.23 = bf16[1,3072,256]{2,1,0:T(8,128)(2,1)S(1)} fusion(f32[1,3072,256]{2,1,0:T(8,128)} %bitcast.67, f32[256]{0:T(256)S(1)} %bitcast.68, bf16[1,3072,256]{2,1,0:T(8,128)(2,1)} %bitcast.45), kind=kLoop, calls=%fused_computation.33 | loop fusion | flops 3932160 | bytes 6292480 | tf_op jit(solution)/shard_map/convert_element_type | solution.py:70
  188.0 17.5 %copy.23 = bf16[1,3072,256]{2,0,1:T(2,128)(2,1)S(1)} copy(bf16[1,3072,256]{2,1,0:T(8,128)(2,1)S(1)} %fusion.23) | data formatting | bytes 3145728 | tf_op jit(solution)/shard_map/convert_element_type | solution.py:70
  205.6 0.5 broadcast.244
  206.1 16.6 %reduce = bf16[3072,256]{1,0:T(8,128)(2,1)} reduce(bf16[3072,1,256]{2,1,0:T(2,128)(2,1)S(1)} %bitcast.65, bf16[]{:T(256)} %broadcast.244), dimensions={1}, to_apply=%bitcast.44.reduce_sub_computation | reduce | bytes 3145730
  222.7 3.7 %reshape.212 = bf16[16,2,24576]{2,1,0:T(2,128)(2,1)S(1)} reshape(bf16[3072,256]{1,0:T(8,128)(2,1)} %reduce) | data formatting | bytes 3145728
  226.5 26.7 %all_to_all.24 = bf16[16,2,24576]{2,1,0:T(2,128)(2,1)} all-to-all(bf16[16,2,24576]{2,1,0:T(2,128)(2,1)S(1)} %reshape.212), channel_id=1, replica_groups=mesh['spec'=16,'tile'=32] {'spec'}, dimensions={0} | all-to-all | bytes 3145728 | tf_op jit(solution)/shard_map/all_to_all | solution.py:98
  253.2 8.1 %reshape.213 = bf16[3072,1,256]{2,1,0:T(2,128)(2,1)S(1)} reshape(bf16[16,2,24576]{2,1,0:T(2,128)(2,1)} %all_to_all.24) | data formatting | bytes 3145728
  261.3 1.4 copy.19
  (42 shorter events, 0.5 us)
Async XLA Ops:
  1.0 13.2 %collective-permute-start = (f32[1,192,256]{2,1,0:T(8,128)S(1)}, f32[1,192,256]{2,1,0:T(8,128)S(1)}, u32[]{:S(2)}, u32[]{:S(2)}) collective-permute-start(f32[1,192,256]{2,1,0:T(8,128)S(1)} %get-tuple-element.105), channel_id=1, source_target_pairs={{0,1},{1,2},{2,3},{3,4},{4,5},{5,6},{6,7},{7,8},{8,9},{9,10},{10,1... | collective-permute-start | bytes 589832 | tf_op jit(solution)/shard_map/ppermute | solution.py:20
  2.9 9.3 %copy-start = (bf16[16,192,256]{2,1,0:T(8,128)(2,1)S(1)}, bf16[16,192,256]{2,1,0:T(8,128)(2,1)}, u32[]{:S(2)}) copy-start(bf16[16,192,256]{2,1,0:T(8,128)(2,1)} %param.8) | copy-start | bytes 4718596
  2.9 11.3 %collective-permute-start.1 = (f32[1,192,256]{2,1,0:T(8,128)S(1)}, f32[1,192,256]{2,1,0:T(8,128)S(1)}, u32[]{:S(2)}, u32[]{:S(2)}) collective-permute-start(f32[1,192,256]{2,1,0:T(8,128)S(1)} %get-tuple-element.106), channel_id=1, source_target_pairs={{1,0},{2,1},{3,2},{4,3},{5,4},{6,5},{7,6},{8,7},{9,8},{10,9},{11,1... | collective-permute-start | bytes 589832 | tf_op jit(solution)/shard_map/ppermute | solution.py:22
  12.2 2.1 copy-start.1
  12.2 2.1 copy-start.2
  20.1 7.0 %collective-permute-start.2 = (f32[1,192,256]{2,1,0:T(8,128)S(1)}, f32[1,192,256]{2,1,0:T(8,128)S(1)}, u32[]{:S(2)}, u32[]{:S(2)}) collective-permute-start(f32[1,192,256]{2,1,0:T(8,128)S(1)} %get-tuple-element.101), channel_id=1, source_target_pairs={{0,1},{1,2},{2,3},{3,4},{4,5},{5,6},{6,7},{7,8},{8,9},{9,10},{10,1... | collective-permute-start | bytes 589832 | tf_op jit(solution)/shard_map/ppermute | solution.py:20
  22.1 6.8 %collective-permute-start.3 = (f32[1,192,256]{2,1,0:T(8,128)S(1)}, f32[1,192,256]{2,1,0:T(8,128)S(1)}, u32[]{:S(2)}, u32[]{:S(2)}) collective-permute-start(f32[1,192,256]{2,1,0:T(8,128)S(1)} %get-tuple-element.102), channel_id=1, source_target_pairs={{1,0},{2,1},{3,2},{4,3},{5,4},{6,5},{7,6},{8,7},{9,8},{10,9},{11,1... | collective-permute-start | bytes 589832 | tf_op jit(solution)/shard_map/ppermute | solution.py:22
  32.8 7.2 %copy-start.3 = (s32[48,24]{0,1:T(8,128)S(1)}, s32[48,24]{0,1:T(8,128)}, u32[]{:S(2)}) copy-start(s32[48,24]{0,1:T(8,128)} %param.12) | copy-start | bytes 13828
  32.8 35.2 %all-to-all-start = ((bf16[16,192,256]{2,1,0:T(8,128)(2,1)}), bf16[16,192,256]{2,1,0:T(8,128)(2,1)}, u32[]{:S(2)}, u32[]{:S(2)}) async-start(bf16[16,192,256]{2,1,0:T(8,128)(2,1)} %fusion.27), calls=%async_computation | async-start | bytes 3145728 | tf_op jit(solution)/shard_map/all_to_all | solution.py:95
where the time goes:
time: 265 us; the launch traced here: 263 us
  local copies, waits for them, and re-layouts  105 us (40%)
  matrix products  50.9 us (19%)
  other arithmetic  32.1 us (12%)
  waiting for transfers between devices  29.2 us (11%)
  blocking collectives  26.7 us (10%)
  starting transfers between devices  18.5 us (7%)
    reshape x6, local copies, waits for them, and re-layouts, advance_group(): assembled = assembled.astype(jnp.bfloat16).reshape(group_size * NF, ND * NF)  45 us
    dot_general x6, matrix products, advance_group(): assembled = jnp.einsum('rjc,rjab->racb', selector, weights)  31.6 us
    all_to_all x1, waiting for transfers between devices, local(): lax.all_to_all(moved, 'spec', split_axis=0, concat_axis=1, tiled=True)  27.2 us
    all_to_all x1, blocking collectives, local(): lax.all_to_all(renewed, 'spec', split_axis=1, concat_axis=0, tiled=True)  26.7 us
    dot_general x6, matrix products, advance_group(): jnp.einsum('ak,rkl->ral', assembled, cell_action, preferred_element_type=...  19.2 us
    convert_element_type x1, local copies, waits for them, and re-layouts, source_update(): return result.astype(jnp.bfloat16)  17.5 us
    gather x12, local copies, waits for them, and re-layouts, advance_group(): weights = table[offsets[group_rows]].astype(jnp.float32)  17.1 us
    unnamed x1, other arithmetic  16.6 us
  transfers between devices with their start and end apart: 5, of which 3 were waited for; matrix products, arithmetic and copies ran while one was open for 4% of the time, Pallas kernels for 0%

commit v1 on v0

--- a/solution.py
+++ b/solution.py
@@ -95,7 +95,10 @@
     incoming = lax.all_to_all(moved, "spec", split_axis=0, concat_axis=1, tiled=True)
     own_mask = lax.dynamic_slice_in_dim(sea_mask, spec_index * share_rows, share_rows, 0)
     renewed = source_update(incoming, own_mask, pattern, table)
-    result = lax.all_to_all(renewed, "spec", split_axis=1, concat_axis=0, tiled=True)
+    result = jnp.concatenate(
+        lax.all_to_all(jnp.stack(jnp.split(renewed, lax.axis_size("spec"), axis=1)), "spec", 0, 0),
+        axis=0,
+    )
     return result
 
 

time: 265 us -> 217 us (0.82)
  the two profiles are of different devices: /device:TPU:320 before, /device:TPU:448 now
where the time goes in v1:
time: 217 us; the launch traced here: 216 us
  local copies, waits for them, and re-layouts  75 us (35%)
  matrix products  50.9 us (23%)
  waiting for transfers between devices  29.2 us (13%)
  blocking collectives  26 us (12%)
  starting transfers between devices  18.5 us (9%)
  other arithmetic  15.5 us (7%)
    reshape x6, local copies, waits for them, and re-layouts, advance_group(): assembled = assembled.astype(jnp.bfloat16).reshape(group_size * NF, ND * NF)  45 us
    dot_general x6, matrix products, advance_group(): assembled = jnp.einsum('rjc,rjab->racb', selector, weights)  31.7 us
    all_to_all x1, waiting for transfers between devices, local(): lax.all_to_all(moved, 'spec', split_axis=0, concat_axis=1, tiled=True)  27.2 us
    all_to_all x1, blocking collectives, local(): lax.all_to_all(jnp.stack(jnp.split(renewed, lax.axis_size('spec'), axis=1...  26 us
    dot_general x6, matrix products, advance_group(): jnp.einsum('ak,rkl->ral', assembled, cell_action, preferred_element_type=...  19.2 us
    gather x12, local copies, waits for them, and re-layouts, advance_group(): weights = table[offsets[group_rows]].astype(jnp.float32)  17.1 us
    ppermute x2, starting transfers between devices, extended(): lax.ppermute(head, axis, [((i + 1) % count, i) for i in range(ends)])  7.42 us
    all_to_all x1, starting transfers between devices, local(): lax.all_to_all(moved, 'spec', split_axis=0, concat_axis=1, tiled=True)  7.21 us
  transfers between devices with their start and end apart: 5, of which 3 were waited for; matrix products, arithmetic and copies ran while one was open for 4% of the time, Pallas kernels for 0%

profile of v1, /device:TPU:448, one launch (start us, length us, event | category | flops | bytes accessed | tf_op | source)
XLA Modules:
  0.0 215.5 jit_solution(1481208219118710369)
XLA Ops:
  0.0 1.0 fusion.58
  1.0 1.9 collective-permute-start
  2.9 0.0 copy-start
  2.9 3.8 %collective-permute-start.1 = (f32[1,192,256]{2,1,0:T(8,128)S(1)}, f32[1,192,256]{2,1,0:T(8,128)S(1)}, u32[]{:S(2)}, u32[]{:S(2)}) collective-permute-start(f32[1,192,256]{2,1,0:T(8,128)S(1)} %get-tuple-element.99), channel_id=1, source_target_pairs={{1,0},{2,1},{3,2},{4,3},{5,4},{6,5},{7,6},{8,7},{9,8},{10,9},{11,1... | collective-permute-start | bytes 589832 | tf_op jit(solution)/shard_map/ppermute | solution.py:22
  6.7 5.5 %fusion.57 = (f32[16,192,255]{2,1,0:T(8,128)}, f32[16,192,255]{2,1,0:T(8,128)}) fusion(bf16[16,192,256]{2,1,0:T(8,128)(2,1)} %param.8), kind=kLoop, calls=%fused_computation.103 | loop fusion | bytes 12533760 | tf_op jit(solution)/shard_map/slice | solution.py:34
  12.2 2.0 convert_element_type.59
  14.2 0.1 sine_multiply_fusion
  14.3 5.8 %fusion.18 = f32[16,192,256]{2,1,0:T(8,128)S(1)} fusion(bf16[16,192,256]{2,1,0:T(8,128)(2,1)S(1)} %copy-done, f32[1,192,256]{2,1,0:T(8,128)S(1)} %collective-permute-done.1, f32[16,192,256]{2,1,0:T(8,128)} %convert_element_type.59, f32[1,192,256]{2,1,0:T(8,128)S(1)} %collective-permute-done, f32[16,192,255]{2,1,0:T(8,128)} %get-tuple-element.97, ...), kind=kLoop, calls=%fused_computation.28 | loop fusion | flops 18087936 | bytes 14558720 | tf_op jit(solution)/shard_map/sub | solution.py:37
  20.2 1.9 collective-permute-start.2
  22.1 3.6 %collective-permute-start.3 = (f32[1,192,256]{2,1,0:T(8,128)S(1)}, f32[1,192,256]{2,1,0:T(8,128)S(1)}, u32[]{:S(2)}, u32[]{:S(2)}) collective-permute-start(f32[1,192,256]{2,1,0:T(8,128)S(1)} %get-tuple-element.95), channel_id=1, source_target_pairs={{1,0},{2,1},{3,2},{4,3},{5,4},{6,5},{7,6},{8,7},{9,8},{10,9},{11,1... | collective-permute-start | bytes 589832 | tf_op jit(solution)/shard_map/ppermute | solution.py:22
  25.7 1.2 fusion.55
  26.9 0.2 collective-permute-done.2
  27.1 1.8 collective-permute-done.3
  28.9 3.9 %fusion.27 = bf16[16,192,256]{2,1,0:T(8,128)(2,1)} fusion(f32[16,192,256]{2,1,0:T(8,128)S(1)} %fusion.18, f32[1,192,256]{2,1,0:T(8,128)S(1)} %collective-permute-done.3, f32[1,192,256]{2,1,0:T(8,128)S(1)} %collective-permute-done.2, f32[16,192,255]{2,1,0:T(8,128)S(1)} %get-tuple-element.93, f32[16,192,255]{2,1,0:T(8,128)S(1)} %get-tuple-element.92, ...), kind=kLoop, calls=%fused_computation.38 | loop fusion | flops 18087936 | bytes 11412992 | tf_op jit(solution)/shard_map/convert_element_type | solution.py:93
  32.8 7.2 %all-to-all-start = ((bf16[16,192,256]{2,1,0:T(8,128)(2,1)}), bf16[16,192,256]{2,1,0:T(8,128)(2,1)}, u32[]{:S(2)}, u32[]{:S(2)}) async-start(bf16[16,192,256]{2,1,0:T(8,128)(2,1)} %fusion.27), calls=%async_computation | async-start | bytes 3145728 | tf_op jit(solution)/shard_map/all_to_all | solution.py:95
  40.1 0.1 copy.26
  40.1 0.7 dynamic-slice_convert_fusion
  40.9 27.2 %all-to-all-done = bf16[16,192,256]{2,1,0:T(8,128)(2,1)} async-done(((bf16[16,192,256]{2,1,0:T(8,128)(2,1)}), bf16[16,192,256]{2,1,0:T(8,128)(2,1)}, u32[]{:S(2)}, u32[]{:S(2)}) %all-to-all-start) | async-done | bytes 1572896 | tf_op jit(solution)/shard_map/all_to_all | solution.py:95
  68.0 117.2 %while.11 = (s32[]{:T(128)}, f32[6,1,512,256]{3,2,1,0:T(8,128)}, s32[6,8]{1,0:T(8,128)S(1)}, s32[48,24]{1,0:T(8,128)S(1)}, bf16[48,64,64]{2,1,0:T(8,128)(2,1)}, ...) while((s32[]{:T(128)}, f32[6,1,512,256]{3,2,1,0:T(8,128)}, ...), condition=%wide.region_1.2_spmd.clone, body=%wide.region_0.1_spmd.clone.sunk | while | flops 882388544 | bytes 19416056 | solution.py:65
  68.1 0.6 gather_fusion
  68.6 0.1 reshape.227
  68.7 2.3 %gather_fusion.1 = bf16[192,64,64]{2,1,0:T(8,128)(2,1)S(1)} fusion(bf16[48,64,64]{2,1,0:T(8,128)(2,1)} %get-tuple-element.165, s32[1024]{0:T(1024)S(1)} %pad_clamp_fusion.5), kind=kCustom, calls=%fused_computation.1.clone.clone.1 | custom fusion | bytes 3146496 | tf_op jit(solution)/shard_map/while/body/eval_jaxpr/gather | solution.py:56
  71.0 0.6 gather_fusion.2
  71.6 5.3 %convert_bitcast_fusion.2 = bf16[8,64,48,64]{3,2,1,0:T(8,128)(2,1)} fusion(bf16[8,24,64,64]{3,2,1,0:T(8,128)(2,1)S(1)} %bitcast.124, s32[8,24]{1,0:T(8,128)S(1)} %gather_fusion.2), kind=kOutput, calls=%fused_computation.4.clone.1 | convolution fusion | flops 77079552 | bytes 4719360 | tf_op jit(solution)/shard_map/while/body/eval_jaxpr/rjc,rjab->racb/dot_general | solution.py:57
  76.9 7.5 %reshape.228 = bf16[512,3072]{1,0:T(8,128)(2,1)S(1)} reshape(bf16[8,64,48,64]{3,2,1,0:T(8,128)(2,1)} %convert_bitcast_fusion.2) | data formatting | bytes 6291456 | tf_op jit(solution)/shard_map/while/body/eval_jaxpr/reshape | solution.py:58
  84.4 3.2 %fusion.71 = f32[6,1,512,256]{3,2,1,0:T(8,128)} fusion(f32[6,1,512,256]{3,2,1,0:T(8,128)} %get-tuple-element.154, s32[]{:T(128)} %get-tuple-element.153, bf16[512,3072]{1,0:T(8,128)(2,1)S(1)} %reshape.228, bf16[1,3072,256]{2,1,0:T(8,128)(2,1)} %get-tuple-element.167), kind=kOutput, calls=%fused_computation.9.clone.1 | convolution fusion | flops 805306368 | bytes 5243392 | tf_op jit(solution)/shard_map/while/body/eval_jaxpr/ak,rkl->ral/dot_general | solution.py:59
  87.6 0.6 gather_fusion
  88.2 0.1 reshape.227
  88.3 2.3 %gather_fusion.1 = bf16[192,64,64]{2,1,0:T(8,128)(2,1)S(1)} fusion(bf16[48,64,64]{2,1,0:T(8,128)(2,1)} %get-tuple-element.165, s32[1024]{0:T(1024)S(1)} %pad_clamp_fusion.5), kind=kCustom, calls=%fused_computation.1.clone.clone.1 | custom fusion | bytes 3146496 | tf_op jit(solution)/shard_map/while/body/eval_jaxpr/gather | solution.py:56
  90.6 0.6 gather_fusion.2
  91.1 5.3 %convert_bitcast_fusion.2 = bf16[8,64,48,64]{3,2,1,0:T(8,128)(2,1)} fusion(bf16[8,24,64,64]{3,2,1,0:T(8,128)(2,1)S(1)} %bitcast.124, s32[8,24]{1,0:T(8,128)S(1)} %gather_fusion.2), kind=kOutput, calls=%fused_computation.4.clone.1 | convolution fusion | flops 77079552 | bytes 4719360 | tf_op jit(solution)/shard_map/while/body/eval_jaxpr/rjc,rjab->racb/dot_general | solution.py:57
  96.4 7.5 %reshape.228 = bf16[512,3072]{1,0:T(8,128)(2,1)S(1)} reshape(bf16[8,64,48,64]{3,2,1,0:T(8,128)(2,1)} %convert_bitcast_fusion.2) | data formatting | bytes 6291456 | tf_op jit(solution)/shard_map/while/body/eval_jaxpr/reshape | solution.py:58
  103.9 3.2 %fusion.71 = f32[6,1,512,256]{3,2,1,0:T(8,128)} fusion(f32[6,1,512,256]{3,2,1,0:T(8,128)} %get-tuple-element.154, s32[]{:T(128)} %get-tuple-element.153, bf16[512,3072]{1,0:T(8,128)(2,1)S(1)} %reshape.228, bf16[1,3072,256]{2,1,0:T(8,128)(2,1)} %get-tuple-element.167), kind=kOutput, calls=%fused_computation.9.clone.1 | convolution fusion | flops 805306368 | bytes 5243392 | tf_op jit(solution)/shard_map/while/body/eval_jaxpr/ak,rkl->ral/dot_general | solution.py:59
  107.1 0.6 gather_fusion
  107.7 0.1 reshape.227
  107.8 2.3 %gather_fusion.1 = bf16[192,64,64]{2,1,0:T(8,128)(2,1)S(1)} fusion(bf16[48,64,64]{2,1,0:T(8,128)(2,1)} %get-tuple-element.165, s32[1024]{0:T(1024)S(1)} %pad_clamp_fusion.5), kind=kCustom, calls=%fused_computation.1.clone.clone.1 | custom fusion | bytes 3146496 | tf_op jit(solution)/shard_map/while/body/eval_jaxpr/gather | solution.py:56
  110.1 0.6 gather_fusion.2
  110.6 5.3 %convert_bitcast_fusion.2 = bf16[8,64,48,64]{3,2,1,0:T(8,128)(2,1)} fusion(bf16[8,24,64,64]{3,2,1,0:T(8,128)(2,1)S(1)} %bitcast.124, s32[8,24]{1,0:T(8,128)S(1)} %gather_fusion.2), kind=kOutput, calls=%fused_computation.4.clone.1 | convolution fusion | flops 77079552 | bytes 4719360 | tf_op jit(solution)/shard_map/while/body/eval_jaxpr/rjc,rjab->racb/dot_general | solution.py:57
  115.9 7.5 %reshape.228 = bf16[512,3072]{1,0:T(8,128)(2,1)S(1)} reshape(bf16[8,64,48,64]{3,2,1,0:T(8,128)(2,1)} %convert_bitcast_fusion.2) | data formatting | bytes 6291456 | tf_op jit(solution)/shard_map/while/body/eval_jaxpr/reshape | solution.py:58
  123.4 3.2 %fusion.71 = f32[6,1,512,256]{3,2,1,0:T(8,128)} fusion(f32[6,1,512,256]{3,2,1,0:T(8,128)} %get-tuple-element.154, s32[]{:T(128)} %get-tuple-element.153, bf16[512,3072]{1,0:T(8,128)(2,1)S(1)} %reshape.228, bf16[1,3072,256]{2,1,0:T(8,128)(2,1)} %get-tuple-element.167), kind=kOutput, calls=%fused_computation.9.clone.1 | convolution fusion | flops 805306368 | bytes 5243392 | tf_op jit(solution)/shard_map/while/body/eval_jaxpr/ak,rkl->ral/dot_general | solution.py:59
  126.6 0.6 gather_fusion
  127.2 0.1 reshape.227
  127.3 2.3 %gather_fusion.1 = bf16[192,64,64]{2,1,0:T(8,128)(2,1)S(1)} fusion(bf16[48,64,64]{2,1,0:T(8,128)(2,1)} %get-tuple-element.165, s32[1024]{0:T(1024)S(1)} %pad_clamp_fusion.5), kind=kCustom, calls=%fused_computation.1.clone.clone.1 | custom fusion | bytes 3146496 | tf_op jit(solution)/shard_map/while/body/eval_jaxpr/gather | solution.py:56
  129.6 0.6 gather_fusion.2
  130.2 5.3 %convert_bitcast_fusion.2 = bf16[8,64,48,64]{3,2,1,0:T(8,128)(2,1)} fusion(bf16[8,24,64,64]{3,2,1,0:T(8,128)(2,1)S(1)} %bitcast.124, s32[8,24]{1,0:T(8,128)S(1)} %gather_fusion.2), kind=kOutput, calls=%fused_computation.4.clone.1 | convolution fusion | flops 77079552 | bytes 4719360 | tf_op jit(solution)/shard_map/while/body/eval_jaxpr/rjc,rjab->racb/dot_general | solution.py:57
  135.4 7.5 %reshape.228 = bf16[512,3072]{1,0:T(8,128)(2,1)S(1)} reshape(bf16[8,64,48,64]{3,2,1,0:T(8,128)(2,1)} %convert_bitcast_fusion.2) | data formatting | bytes 6291456 | tf_op jit(solution)/shard_map/while/body/eval_jaxpr/reshape | solution.py:58
  143.0 3.2 %fusion.71 = f32[6,1,512,256]{3,2,1,0:T(8,128)} fusion(f32[6,1,512,256]{3,2,1,0:T(8,128)} %get-tuple-element.154, s32[]{:T(128)} %get-tuple-element.153, bf16[512,3072]{1,0:T(8,128)(2,1)S(1)} %reshape.228, bf16[1,3072,256]{2,1,0:T(8,128)(2,1)} %get-tuple-element.167), kind=kOutput, calls=%fused_computation.9.clone.1 | convolution fusion | flops 805306368 | bytes 5243392 | tf_op jit(solution)/shard_map/while/body/eval_jaxpr/ak,rkl->ral/dot_general | solution.py:59
  146.2 0.6 gather_fusion
  146.8 0.1 reshape.227
  146.9 2.3 %gather_fusion.1 = bf16[192,64,64]{2,1,0:T(8,128)(2,1)S(1)} fusion(bf16[48,64,64]{2,1,0:T(8,128)(2,1)} %get-tuple-element.165, s32[1024]{0:T(1024)S(1)} %pad_clamp_fusion.5), kind=kCustom, calls=%fused_computation.1.clone.clone.1 | custom fusion | bytes 3146496 | tf_op jit(solution)/shard_map/while/body/eval_jaxpr/gather | solution.py:56
  149.2 0.6 gather_fusion.2
  149.7 5.3 %convert_bitcast_fusion.2 = bf16[8,64,48,64]{3,2,1,0:T(8,128)(2,1)} fusion(bf16[8,24,64,64]{3,2,1,0:T(8,128)(2,1)S(1)} %bitcast.124, s32[8,24]{1,0:T(8,128)S(1)} %gather_fusion.2), kind=kOutput, calls=%fused_computation.4.clone.1 | convolution fusion | flops 77079552 | bytes 4719360 | tf_op jit(solution)/shard_map/while/body/eval_jaxpr/rjc,rjab->racb/dot_general | solution.py:57
  155.0 7.5 %reshape.228 = bf16[512,3072]{1,0:T(8,128)(2,1)S(1)} reshape(bf16[8,64,48,64]{3,2,1,0:T(8,128)(2,1)} %convert_bitcast_fusion.2) | data formatting | bytes 6291456 | tf_op jit(solution)/shard_map/while/body/eval_jaxpr/reshape | solution.py:58
  162.5 3.2 %fusion.71 = f32[6,1,512,256]{3,2,1,0:T(8,128)} fusion(f32[6,1,512,256]{3,2,1,0:T(8,128)} %get-tuple-element.154, s32[]{:T(128)} %get-tuple-element.153, bf16[512,3072]{1,0:T(8,128)(2,1)S(1)} %reshape.228, bf16[1,3072,256]{2,1,0:T(8,128)(2,1)} %get-tuple-element.167), kind=kOutput, calls=%fused_computation.9.clone.1 | convolution fusion | flops 805306368 | bytes 5243392 | tf_op jit(solution)/shard_map/while/body/eval_jaxpr/ak,rkl->ral/dot_general | solution.py:59
  165.8 0.6 gather_fusion
  166.3 0.1 reshape.227
  166.4 2.3 %gather_fusion.1 = bf16[192,64,64]{2,1,0:T(8,128)(2,1)S(1)} fusion(bf16[48,64,64]{2,1,0:T(8,128)(2,1)} %get-tuple-element.165, s32[1024]{0:T(1024)S(1)} %pad_clamp_fusion.5), kind=kCustom, calls=%fused_computation.1.clone.clone.1 | custom fusion | bytes 3146496 | tf_op jit(solution)/shard_map/while/body/eval_jaxpr/gather | solution.py:56
  168.7 0.6 gather_fusion.2
  169.3 5.3 %convert_bitcast_fusion.2 = bf16[8,64,48,64]{3,2,1,0:T(8,128)(2,1)} fusion(bf16[8,24,64,64]{3,2,1,0:T(8,128)(2,1)S(1)} %bitcast.124, s32[8,24]{1,0:T(8,128)S(1)} %gather_fusion.2), kind=kOutput, calls=%fused_computation.4.clone.1 | convolution fusion | flops 77079552 | bytes 4719360 | tf_op jit(solution)/shard_map/while/body/eval_jaxpr/rjc,rjab->racb/dot_general | solution.py:57
  174.6 7.5 %reshape.228 = bf16[512,3072]{1,0:T(8,128)(2,1)S(1)} reshape(bf16[8,64,48,64]{3,2,1,0:T(8,128)(2,1)} %convert_bitcast_fusion.2) | data formatting | bytes 6291456 | tf_op jit(solution)/shard_map/while/body/eval_jaxpr/reshape | solution.py:58
  182.1 3.2 %fusion.71 = f32[6,1,512,256]{3,2,1,0:T(8,128)} fusion(f32[6,1,512,256]{3,2,1,0:T(8,128)} %get-tuple-element.154, s32[]{:T(128)} %get-tuple-element.153, bf16[512,3072]{1,0:T(8,128)(2,1)S(1)} %reshape.228, bf16[1,3072,256]{2,1,0:T(8,128)(2,1)} %get-tuple-element.167), kind=kOutput, calls=%fused_computation.9.clone.1 | convolution fusion | flops 805306368 | bytes 5243392 | tf_op jit(solution)/shard_map/while/body/eval_jaxpr/ak,rkl->ral/dot_general | solution.py:59
  185.3 2.8 %fusion.23 = bf16[1,3072,256]{2,1,0:T(8,128)(2,1)S(1)} fusion(f32[1,3072,256]{2,1,0:T(8,128)} %bitcast.126, f32[256]{0:T(256)S(1)} %bitcast.127, bf16[1,3072,256]{2,1,0:T(8,128)(2,1)} %bitcast.105), kind=kLoop, calls=%fused_computation.33 | loop fusion | flops 3932160 | bytes 6292480 | tf_op jit(solution)/shard_map/convert_element_type | solution.py:70
  188.4 26.0 %all_to_all.17 = bf16[16,1,192,256]{3,2,1,0:T(8,128)(2,1)S(1)} all-to-all(bf16[16,1,192,256]{3,2,1,0:T(8,128)(2,1)S(1)} %fusion.35), channel_id=1, replica_groups=mesh['spec'=16,'tile'=32] {'spec'}, dimensions={0} | all-to-all | bytes 3145728 | tf_op jit(solution)/shard_map/all_to_all | solution.py:99
  214.4 1.1 copy.57
  (53 shorter events, 0.4 us)
Async XLA Ops:
  1.0 13.3 %collective-permute-start = (f32[1,192,256]{2,1,0:T(8,128)S(1)}, f32[1,192,256]{2,1,0:T(8,128)S(1)}, u32[]{:S(2)}, u32[]{:S(2)}) collective-permute-start(f32[1,192,256]{2,1,0:T(8,128)S(1)} %get-tuple-element.98), channel_id=1, source_target_pairs={{0,1},{1,2},{2,3},{3,4},{4,5},{5,6},{6,7},{7,8},{8,9},{9,10},{10,1... | collective-permute-start | bytes 589832 | tf_op jit(solution)/shard_map/ppermute | solution.py:20
  2.9 9.3 %copy-start = (bf16[16,192,256]{2,1,0:T(8,128)(2,1)S(1)}, bf16[16,192,256]{2,1,0:T(8,128)(2,1)}, u32[]{:S(2)}) copy-start(bf16[16,192,256]{2,1,0:T(8,128)(2,1)} %param.8) | copy-start | bytes 4718596
  2.9 11.3 %collective-permute-start.1 = (f32[1,192,256]{2,1,0:T(8,128)S(1)}, f32[1,192,256]{2,1,0:T(8,128)S(1)}, u32[]{:S(2)}, u32[]{:S(2)}) collective-permute-start(f32[1,192,256]{2,1,0:T(8,128)S(1)} %get-tuple-element.99), channel_id=1, source_target_pairs={{1,0},{2,1},{3,2},{4,3},{5,4},{6,5},{7,6},{8,7},{9,8},{10,9},{11,1... | collective-permute-start | bytes 589832 | tf_op jit(solution)/shard_map/ppermute | solution.py:22
  12.2 2.1 copy-start.1
  12.2 2.1 copy-start.2
  20.2 7.0 %collective-permute-start.2 = (f32[1,192,256]{2,1,0:T(8,128)S(1)}, f32[1,192,256]{2,1,0:T(8,128)S(1)}, u32[]{:S(2)}, u32[]{:S(2)}) collective-permute-start(f32[1,192,256]{2,1,0:T(8,128)S(1)} %get-tuple-element.94), channel_id=1, source_target_pairs={{0,1},{1,2},{2,3},{3,4},{4,5},{5,6},{6,7},{7,8},{8,9},{9,10},{10,1... | collective-permute-start | bytes 589832 | tf_op jit(solution)/shard_map/ppermute | solution.py:20
  22.1 6.8 %collective-permute-start.3 = (f32[1,192,256]{2,1,0:T(8,128)S(1)}, f32[1,192,256]{2,1,0:T(8,128)S(1)}, u32[]{:S(2)}, u32[]{:S(2)}) collective-permute-start(f32[1,192,256]{2,1,0:T(8,128)S(1)} %get-tuple-element.95), channel_id=1, source_target_pairs={{1,0},{2,1},{3,2},{4,3},{5,4},{6,5},{7,6},{8,7},{9,8},{10,9},{11,1... | collective-permute-start | bytes 589832 | tf_op jit(solution)/shard_map/ppermute | solution.py:22
  32.8 7.2 %copy-start.3 = (s32[48,24]{0,1:T(8,128)S(1)}, s32[48,24]{0,1:T(8,128)}, u32[]{:S(2)}) copy-start(s32[48,24]{0,1:T(8,128)} %param.12) | copy-start | bytes 13828
  32.8 35.2 %all-to-all-start = ((bf16[16,192,256]{2,1,0:T(8,128)(2,1)}), bf16[16,192,256]{2,1,0:T(8,128)(2,1)}, u32[]{:S(2)}, u32[]{:S(2)}) async-start(bf16[16,192,256]{2,1,0:T(8,128)(2,1)} %fusion.27), calls=%async_computation | async-start | bytes 3145728 | tf_op jit(solution)/shard_map/all_to_all | solution.py:95
